TPU v7x, 32 devices: a whole 2x2x4 slice. The times are simulated.
32 devices in a mesh: row: 8 (over z, y), col: 4 (over x, core).
Axes of the slice: x: 2, y: 2, z: 4, core: 2. Of those that a mesh axis runs over, the one named last changes fastest.
Arguments:
- tensor: bfloat16 [1024, 64, 512], P('row', None, 'col'), may hold values from -6 to 6
- loss_kind: int32 [1024, 64, 512], P('row', None, 'col'), may hold values from 0 to 1, as said below
- factor_one: float32 [1024, 512], P(('row', 'col')), may hold values from -2 to 2
- factor_two: float32 [512, 512], P(('col', 'row')), may hold values from -2 to 2
- factor_three: float32 [64, 512], replicated, may hold values from -2 to 2
- first_one: float32 [1024, 512], P(('row', 'col')), may hold values from -0.03 to 0.03
- second_one: float32 [1024, 512], P(('row', 'col')), may hold values from 0.0005 to 0.05
- first_two: float32 [512, 512], P(('col', 'row')), may hold values from -0.03 to 0.03
- second_two: float32 [512, 512], P(('col', 'row')), may hold values from 0.0005 to 0.05
- first_three: float32 [64, 512], replicated, may hold values from -0.03 to 0.03
- second_three: float32 [64, 512], replicated, may hold values from 0.0005 to 0.05
Outputs:
- new_one: float32 [1024, 512], P(('row', 'col'))
- new_two: float32 [512, 512], P(('col', 'row'))
- new_three: float32 [64, 512], replicated
Inputs may be any that keep to these rules, and one draw needn't show every extreme that they name: loss_kind takes one value on each block of 128 first-mode by 128 second-mode indices (with all 64 third-mode ones), aligned to multiples of 128 and 128, and is 1 on exactly half of these blocks.
All inputs are finite; a program needn't handle non-finite values.
Results may differ from a plain program's by a relative error of at most 0.003.
Values may be sent and summed in bfloat16 or wider, within the bound.
A program may use at most 128 MiB of HBM per device.

v0:
```python
import math

import jax
import jax.numpy as jnp
from jax import lax
from jax.sharding import PartitionSpec as P

ITERS = 2
STEP = 10


learn_rate = 0.05
beta_one = 0.8
beta_two = 0.95
adam_eps = 1e-08


def loss_slope(rebuilt, values, kinds):
    excess = rebuilt - values
    huber_part = jnp.clip(excess, -1.0, 1.0)
    target = jnp.where(values > 0, 1.0, 0.0).astype(rebuilt.dtype)
    logit_part = jax.nn.sigmoid(rebuilt) - target
    return jnp.where(kinds == 1, logit_part, huber_part)


def adam_step(param, first, second, grad, counter):
    first = beta_one * first + (1.0 - beta_one) * grad
    second = beta_two * second + (1.0 - beta_two) * grad * grad
    corr_one = 1.0 - beta_one**counter
    corr_two = 1.0 - beta_two**counter
    param = param - learn_rate * (first / corr_one) / (jnp.sqrt(second / corr_two) + adam_eps)
    return (param, first, second)


def tile_grads(tensor, loss_kind, half_one, half_two, half_three, scales):
    tile_rows, tile_depth, tile_cols = tensor.shape
    rank_width = half_one.shape[1]
    one_f = half_one.astype(jnp.float32)
    three_f = half_three.astype(jnp.float32)
    scaled_rows = (
        (one_f[:, None, :] * three_f[None, :, :])
        .astype(jnp.bfloat16)
        .reshape(tile_rows * tile_depth, rank_width)
    )
    rebuilt = lax.dot_general(
        scaled_rows, half_two, (((1,), (1,)), ((), ())), preferred_element_type=jnp.float32
    )
    values = tensor.reshape(tile_rows * tile_depth, tile_cols).astype(jnp.float32)
    deriv_bf = loss_slope(
        rebuilt, values, loss_kind.reshape(tile_rows * tile_depth, tile_cols)
    ).astype(jnp.bfloat16)
    projected = jnp.dot(deriv_bf, half_two, preferred_element_type=jnp.float32).reshape(
        tile_rows, tile_depth, rank_width
    )
    grad_one = jnp.sum(projected * three_f[None, :, :], axis=1) * scales[0]
    grad_three = jnp.sum(projected * one_f[:, None, :], axis=0) * scales[2]
    grad_two = (
        lax.dot_general(
            deriv_bf, scaled_rows, (((0,), (0,)), ((), ())), preferred_element_type=jnp.float32
        )
        * scales[1]
    )
    return (grad_one, grad_two, grad_three)


def third_sum(grad_three):
    return lax.psum(grad_three, ("row", "col"))


def shards(
    tensor,
    loss_kind,
    factor_one,
    factor_two,
    factor_three,
    first_one,
    second_one,
    first_two,
    second_two,
    first_three,
    second_three,
):
    tile_rows, tile_depth, tile_cols = tensor.shape
    full_rows = tile_rows * lax.axis_size("row")
    full_cols = tile_cols * lax.axis_size("col")
    scales = (
        1.0 / math.sqrt(full_cols * tile_depth),
        1.0 / math.sqrt(full_rows * tile_depth),
        1.0 / math.sqrt(full_rows * full_cols),
    )
    start_one, start_two, start_three = (factor_one, factor_two, factor_three)
    for iteration in range(ITERS):
        half_one = lax.all_gather(factor_one.astype(jnp.bfloat16), "col", axis=0, tiled=True)
        half_two = lax.all_gather(factor_two.astype(jnp.bfloat16), "row", axis=0, tiled=True)
        grad_one, grad_two, grad_three = tile_grads(
            tensor, loss_kind, half_one, half_two, factor_three.astype(jnp.bfloat16), scales
        )
        grad_one = lax.psum_scatter(grad_one, "col", scatter_dimension=0, tiled=True)
        grad_two = lax.psum_scatter(grad_two, "row", scatter_dimension=0, tiled=True)
        grad_three = third_sum(grad_three)
        counter = STEP + iteration + 1
        factor_one, first_one, second_one = adam_step(
            factor_one, first_one, second_one, grad_one, counter
        )
        factor_two, first_two, second_two = adam_step(
            factor_two, first_two, second_two, grad_two, counter
        )
        factor_three, first_three, second_three = adam_step(
            factor_three, first_three, second_three, grad_three, counter
        )
    spread = learn_rate * ITERS
    return (
        (start_one - factor_one) / spread,
        (start_two - factor_two) / spread,
        (start_three - factor_three) / spread,
    )


def solution(mesh):
    in_specs = (
        P("row", None, "col"),
        P("row", None, "col"),
        P(("row", "col"), None),
        P(("col", "row"), None),
        P(),
        P(("row", "col"), None),
        P(("row", "col"), None),
        P(("col", "row"), None),
        P(("col", "row"), None),
        P(),
        P(),
    )
    out_specs = (P(("row", "col"), None), P(("col", "row"), None), P())
    return jax.shard_map(shards, mesh=mesh, in_specs=in_specs, out_specs=out_specs, check_vma=False)
```

profile of v0, /device:TPU:0, one launch (start us, length us, event | category | flops | bytes accessed | tf_op | source)
XLA Modules:
  0.0 399.3 jit_solution(8798334853152890748)
XLA Ops:
  8.0 0.0 all-reduce.3.cloned.1.call-start
  8.0 0.8 convert_element_type.63
  8.8 0.8 convert_element_type.57
  9.7 6.5 %all_gather.12 = bf16[128,512]{1,0:T(8,128)(2,1)S(1)} all-gather(bf16[32,512]{1,0:T(8,128)(2,1)S(1)} %convert_element_type.57), channel_id=1, replica_groups=mesh['row'=8,'col'=4] {'col'}, dimensions={0}, use_global_device_ids=true | all-gather | bytes 163840 | tf_op jit(solution)/shard_map/all_gather | solution.py:93
  16.1 31.3 %all_gather.13 = bf16[128,512]{1,0:T(8,128)(2,1)S(1)} all-gather(bf16[16,512]{1,0:T(8,128)(2,1)S(1)} %convert_element_type.63), channel_id=1, replica_groups=mesh['row'=8,'col'=4] {'row'}, dimensions={0}, use_global_device_ids=true | all-gather | bytes 147456 | tf_op jit(solution)/shard_map/all_gather | solution.py:94
  47.4 0.9 convert_convert_fusion
  48.3 2.8 broadcast_compare_fusion
  51.1 0.0 copy-start.17
  51.1 3.3 multiply_convert_fusion.1
  54.5 2.4 fusion.1
  56.9 0.8 copy-done.1
  57.7 8.1 %multiply_reduce_fusion.3 = (f32[128,512]{1,0:T(8,128)S(1)}, f32[8192,512]{1,0:T(8,128)}) fusion(f32[64,512]{1,0:T(8,128)S(1)} %convert_convert_fusion, bf16[8192,128]{1,0:T(8,128)(2,1)S(1)} %fusion.1, bf16[128,512]{1,0:T(8,128)(2,1)S(1)} %all_gather.13), kind=kOutput, calls=%fused_computation.4 | convolution fusion | flops 1082064896 | bytes 19398656 | tf_op jit(solution)/shard_map/dot_general | solution.py:52
  65.8 8.4 %multiply_reduce_fusion.2 = f32[64,512]{1,0:T(8,128)S(1)} fusion(f32[128,64,512]{2,1,0:T(8,128)} %bitcast.30, f32[128,512]{1,0:T(8,128)S(1)} %convert_element_type.58), kind=kLoop, calls=%fused_computation.3 | loop fusion | flops 8355840 | bytes 17170432 | tf_op jit(solution)/shard_map/reduce_sum | solution.py:56
  74.2 0.7 broadcast_multiply_fusion.3
  74.9 0.0 all-reduce.3.cloned.1.call-update
  74.9 0.0 copy-start.7
  74.9 0.0 copy-start.9
  75.0 0.0 reduce-scatter.7.cloned.1.call-start
  75.1 5.5 %convolution_multiply_fusion.1 = f32[128,512]{1,0:T(8,128)} fusion(bf16[8192,128]{1,0:T(8,128)(2,1)S(1)} %fusion.1, bf16[8192,512]{1,0:T(8,128)(2,1)} %bitcast.35), kind=kOutput, calls=%fused_computation.19 | convolution fusion | flops 1073807360 | bytes 10747904 | tf_op jit(solution)/shard_map/dot_general | solution.py:58
  80.6 0.0 reduce-scatter.7.cloned.1.call-update
  80.6 0.0 reduce-scatter.5.cloned.1.call-start
  80.7 0.7 broadcast_multiply_fusion.1
  81.4 0.0 reduce-scatter.5.cloned.1.call-update
  81.4 0.0 all-reduce.5.cloned.1.call-start
  81.5 119.0 %all-reduce.3.cloned.1.call-done = f32[64,512]{1,0:T(8,128)} async-done(((f32[64,512]{1,0:T(8,128)}), f32[64,512]{1,0:T(8,128)}) %all-reduce.3.cloned.1.call-update) | async-done | bytes 131088 | tf_op jit(solution)/shard_map/psum | solution.py:67
  200.5 1.0 fusion.24
  201.5 0.0 reduce-scatter.7.cloned.1.call-done
  201.6 0.8 fusion.36
  202.4 30.5 %all_gather.15 = bf16[128,512]{1,0:T(8,128)(2,1)S(1)} all-gather(bf16[16,512]{1,0:T(8,128)(2,1)S(1)} %fusion.36), channel_id=1, replica_groups=mesh['row'=8,'col'=4] {'row'}, dimensions={0}, use_global_device_ids=true | all-gather | bytes 147456 | tf_op jit(solution)/shard_map/all_gather | solution.py:94
  232.9 0.9 fusion.26
  233.8 5.6 %all_gather.14 = bf16[128,512]{1,0:T(8,128)(2,1)S(1)} all-gather(bf16[32,512]{1,0:T(8,128)(2,1)S(1)} %fusion.26), channel_id=1, replica_groups=mesh['row'=8,'col'=4] {'col'}, dimensions={0}, use_global_device_ids=true | all-gather | bytes 163840 | tf_op jit(solution)/shard_map/all_gather | solution.py:93
  239.4 3.3 multiply_convert_fusion
  242.8 2.4 fusion.3
  245.2 0.8 copy-done
  246.0 8.1 %multiply_reduce_fusion.1 = (f32[128,512]{1,0:T(8,128)S(1)}, f32[8192,512]{1,0:T(8,128)}) fusion(f32[64,512]{1,0:T(8,128)S(1)} %fusion.24, bf16[8192,128]{1,0:T(8,128)(2,1)S(1)} %fusion.3, bf16[128,512]{1,0:T(8,128)(2,1)S(1)} %all_gather.15), kind=kOutput, calls=%fused_computation.1 | convolution fusion | flops 1082064896 | bytes 19398656 | tf_op jit(solution)/shard_map/dot_general | solution.py:52
  254.1 8.4 %multiply_reduce_fusion = f32[64,512]{1,0:T(8,128)S(1)} fusion(f32[128,64,512]{2,1,0:T(8,128)} %bitcast.31, f32[128,512]{1,0:T(8,128)S(1)} %convert_element_type.68), kind=kLoop, calls=%fused_computation | loop fusion | flops 8355840 | bytes 17170432 | tf_op jit(solution)/shard_map/reduce_sum | solution.py:56
  262.5 0.7 broadcast_multiply_fusion.2
  263.2 0.0 all-reduce.5.cloned.1.call-update
  263.2 0.0 reduce-scatter.11.cloned.1.call-start
  263.3 5.4 %convolution_multiply_fusion = f32[128,512]{1,0:T(8,128)} fusion(bf16[8192,128]{1,0:T(8,128)(2,1)S(1)} %fusion.3, bf16[8192,512]{1,0:T(8,128)(2,1)} %bitcast.33), kind=kOutput, calls=%fused_computation.18 | convolution fusion | flops 1073807360 | bytes 10747904 | tf_op jit(solution)/shard_map/dot_general | solution.py:58
  268.7 0.0 reduce-scatter.11.cloned.1.call-update
  268.7 0.0 reduce-scatter.9.cloned.1.call-start
  268.8 0.7 broadcast_multiply_fusion
  269.5 0.0 reduce-scatter.9.cloned.1.call-update
  269.5 117.4 %all-reduce.5.cloned.1.call-done = f32[64,512]{1,0:T(8,128)} async-done(((f32[64,512]{1,0:T(8,128)}), f32[64,512]{1,0:T(8,128)}) %all-reduce.5.cloned.1.call-update) | async-done | bytes 131088 | tf_op jit(solution)/shard_map/psum | solution.py:67
  386.9 1.7 fusion.14
  388.7 1.4 fusion.35
  390.1 1.6 fusion.25
  (38 shorter events, 0.1 us)
Async XLA Ops:
  8.0 192.5 %all-reduce.3.cloned.1.call-start = ((), (), s32[]{:S(2)}) async-start(), calls=%async_computation.5 | async-start | bytes 262144 | tf_op jit(solution)/shard_map/psum | solution.py:67
  51.1 3.4 copy-start.3
  51.1 3.4 copy-start.17
  54.5 3.2 copy-start.1
  74.9 125.6 %copy-start.2 = (f32[64,512]{1,0:T(8,128)S(1)}, f32[64,512]{1,0:T(8,128)}, u32[]{:S(2)}) copy-start(f32[64,512]{1,0:T(8,128)} %param.15) | copy-start | bytes 393220
  74.9 125.6 %copy-start.6 = (f32[64,512]{1,0:T(8,128)S(1)}, f32[64,512]{1,0:T(8,128)}, u32[]{:S(2)}) copy-start(f32[64,512]{1,0:T(8,128)} %param.20) | copy-start | bytes 393220
  74.9 125.6 %copy-start.7 = (f32[64,512]{1,0:T(8,128)S(1)}, f32[64,512]{1,0:T(8,128)}, u32[]{:S(2)}) copy-start(f32[64,512]{1,0:T(8,128)} %param.21) | copy-start | bytes 393220
  74.9 126.6 %copy-start.9 = (f32[16,512]{1,0:T(8,128)S(1)}, f32[16,512]{1,0:T(8,128)}, u32[]{:S(2)}) copy-start(f32[16,512]{1,0:T(8,128)} %param.14) | copy-start | bytes 98308
  75.0 126.6 %copy-start.13 = (f32[16,512]{1,0:T(8,128)S(1)}, f32[16,512]{1,0:T(8,128)}, u32[]{:S(2)}) copy-start(f32[16,512]{1,0:T(8,128)} %param.18) | copy-start | bytes 98308
  75.0 126.6 %copy-start.14 = (f32[16,512]{1,0:T(8,128)S(1)}, f32[16,512]{1,0:T(8,128)}, u32[]{:S(2)}) copy-start(f32[16,512]{1,0:T(8,128)} %param.19) | copy-start | bytes 98308
  75.0 157.9 %copy-start.5 = (f32[32,512]{1,0:T(8,128)S(1)}, f32[32,512]{1,0:T(8,128)}, u32[]{:S(2)}) copy-start(f32[32,512]{1,0:T(8,128)} %param.13) | copy-start | bytes 196612
  75.0 157.9 %copy-start.10 = (f32[32,512]{1,0:T(8,128)S(1)}, f32[32,512]{1,0:T(8,128)}, u32[]{:S(2)}) copy-start(f32[32,512]{1,0:T(8,128)} %param.16) | copy-start | bytes 196612
  75.0 157.9 %copy-start.11 = (f32[32,512]{1,0:T(8,128)S(1)}, f32[32,512]{1,0:T(8,128)}, u32[]{:S(2)}) copy-start(f32[32,512]{1,0:T(8,128)} %param.17) | copy-start | bytes 196612
  75.0 126.5 %reduce-scatter.7.cloned.1.call-start = ((), (), s32[]{:S(2)}) async-start(), calls=%async_computation.6 | async-start | bytes 294912 | tf_op jit(solution)/shard_map/reduce_scatter | solution.py:99
  80.6 152.3 %reduce-scatter.5.cloned.1.call-start = ((), (), s32[]{:S(2)}) async-start(), calls=%async_computation.4 | async-start | bytes 327680 | tf_op jit(solution)/shard_map/reduce_scatter | solution.py:98
  81.4 305.5 %all-reduce.5.cloned.1.call-start = ((), (), s32[]{:S(2)}) async-start(), calls=%async_computation.9 | async-start | bytes 262144 | tf_op jit(solution)/shard_map/psum | solution.py:67
  239.4 3.4 copy-start.4
  239.4 3.4 copy-start.18
  242.8 3.2 copy-start
  263.2 123.7 %copy-start.8 = (f32[64,512]{1,0:T(8,128)S(1)}, f32[64,512]{1,0:T(8,128)}, u32[]{:S(2)}) copy-start(f32[64,512]{1,0:T(8,128)} %all-reduce.3.cloned.1.call-done) | copy-start | bytes 393220
  263.2 125.5 %copy-start.15 = (f32[16,512]{1,0:T(8,128)S(1)}, f32[16,512]{1,0:T(8,128)}, u32[]{:S(2)}) copy-start(f32[16,512]{1,0:T(8,128)} %param.19) | copy-start | bytes 98308
  263.2 125.5 %copy-start.16 = (f32[16,512]{1,0:T(8,128)S(1)}, f32[16,512]{1,0:T(8,128)}, u32[]{:S(2)}) copy-start(f32[16,512]{1,0:T(8,128)} %reduce-scatter.7.cloned.1.call-done) | copy-start | bytes 98308
  263.2 126.9 %copy-start.12 = (f32[32,512]{1,0:T(8,128)S(1)}, f32[32,512]{1,0:T(8,128)}, u32[]{:S(2)}) copy-start(f32[32,512]{1,0:T(8,128)} %reduce-scatter.5.cloned.1.call-done) | copy-start | bytes 196612
  263.2 125.4 %reduce-scatter.11.cloned.1.call-start = ((), (), s32[]{:S(2)}) async-start(), calls=%async_computation.8 | async-start | bytes 294912 | tf_op jit(solution)/shard_map/reduce_scatter | solution.py:99
  268.7 121.4 %reduce-scatter.9.cloned.1.call-start = ((), (), s32[]{:S(2)}) async-start(), calls=%async_computation.7 | async-start | bytes 327680 | tf_op jit(solution)/shard_map/reduce_scatter | solution.py:98
Sparse Core Ops, SparseCore 0:
  75.0 125.4 all-reduce.2
  263.3 123.5 all-reduce.4
Sparse Core Ops, SparseCore 1:
  80.7 63.0 reduce-scatter.6
  146.1 19.0 reduce-scatter.4
  268.8 61.1 reduce-scatter.10
  332.5 19.0 reduce-scatter.8
where the time goes:
time: 400 us; the launch traced here: 399 us
  waiting for transfers between devices  237 us (59%)
  blocking collectives  73.9 us (18%)
  other arithmetic  39.1 us (10%)
  matrix products  31.8 us (8%)
  between operations  16 us (4%)
    psum x2, waiting for transfers between devices, third_sum(): return lax.psum(grad_three, ('row', 'col'))  236 us
    all_gather x2, blocking collectives, shards(): lax.all_gather(factor_two.astype(jnp.bfloat16), 'row', axis=0, tiled=True)  61.8 us
    reduce_sum x2, other arithmetic, tile_grads(): grad_three = jnp.sum(projected * one_f[:, None, :], axis=0) * scales[2]  16.8 us
    dot_general x2, matrix products, tile_grads(): jnp.dot(deriv_bf, half_two, preferred_element_type=jnp.float32)  16.2 us
    all_gather x2, blocking collectives, shards(): lax.all_gather(factor_one.astype(jnp.bfloat16), 'col', axis=0, tiled=True)  12.1 us
    dot_general x2, matrix products, tile_grads(): lax.dot_general(deriv_bf, scaled_rows, (((0,), (0,)), ((), ())), preferre...  10.9 us
  transfers between devices with their start and end apart: 6, of which 2 were waited for; matrix products, arithmetic and copies ran while one was open for 4% of the time, Pallas kernels for 0%

commit v1 on v0

v1 whole, which is shorter than its diff:
```python
import functools
import math

import jax
import jax.numpy as jnp
from jax import lax
from jax.experimental import pallas as pl
from jax.experimental.pallas import tpu as pltpu
from jax.sharding import PartitionSpec as P

ITERS = 2
STEP = 10
BLOCK = 8
LANES = 128

learn_rate = 0.05
beta_one = 0.8
beta_two = 0.95
adam_eps = 1e-08

F32 = jnp.float32
BF16 = jnp.bfloat16


def adam_step(param, first, second, grad, counter):
    first = beta_one * first + (1.0 - beta_one) * grad
    second = beta_two * second + (1.0 - beta_two) * grad * grad
    corr_one = 1.0 - beta_one**counter
    corr_two = 1.0 - beta_two**counter
    param = param - learn_rate * (first / corr_one) / (jnp.sqrt(second / corr_two) + adam_eps)
    return (param, first, second)


def kernel(
    n_row, n_col, scales,
    tensor, kind, a_in, b_in, c_in, ma_in, va_in, mb_in, vb_in, mc_in, vc_in,
    oa, ob, oc,
    x_s, kind_s, ag_a, ag_b, ag_c, gs_a, gs_b, gs_c, rs_a, rs_b, rs_c,
    a_f, bt, c_f, ga, gb, gc, st_a, st_b, st_c, split,
    load_sem, sends, recvs,
):
    row = lax.axis_index("row")
    col = lax.axis_index("col")
    n_all = n_row * n_col
    me = row * n_col + col
    tile_rows, depth, tile_cols = x_s.shape
    rank = a_f.shape[1]
    own_a = a_in.shape[0]
    own_b = b_in.shape[0]
    chunk = st_c.shape[1]
    groups = rank // LANES

    load_x = pltpu.make_async_copy(tensor, x_s, load_sem.at[0])
    load_x.start()
    load_k = pltpu.make_async_copy(kind.at[0, pl.ds(0, 8)], kind_s, load_sem.at[1])
    load_k.start()

    barrier = pltpu.get_barrier_semaphore()

    def device(d):
        return {"row": lax.div(d, n_col), "col": lax.rem(d, n_col)}

    def greet(k, carry):
        pl.semaphore_signal(
            barrier, inc=1, device_id=device(lax.rem(me + k, n_all)),
            device_id_type=pl.DeviceIdType.MESH,
        )
        return carry

    lax.fori_loop(1, n_all, greet, 0)

    kinds = {
        "a": (n_col, col, lambda d: {"col": d}, 0),
        "b": (n_row, row, lambda d: {"row": d}, 1),
        "c": (n_all, me, device, 2),
    }

    def copy(src, dst, what, slot, target):
        return pltpu.make_async_remote_copy(
            src_ref=src, dst_ref=dst, send_sem=sends.at[slot], recv_sem=recvs.at[slot],
            device_id=kinds[what][2](target), device_id_type=pl.DeviceIdType.MESH,
        )

    def slot_of(what, it, phase):
        return (kinds[what][3] * 2 + phase) * (ITERS + 1) + it

    def send_all(what, it, phase, src, dst):
        n, mine, _, _ = kinds[what]

        def body(k, carry):
            peer = lax.rem(mine + k, n)
            source = src.at[it, mine] if phase == 0 else src.at[it, peer]
            copy(source, dst.at[it, mine], what, slot_of(what, it, phase), peer).start()
            return carry

        lax.fori_loop(1, n, body, 0)

    def whole(what, it, phase, src, dst):
        n, mine, _, _ = kinds[what]
        part = pl.ds(0, n - 1)
        return copy(
            src.at[it, part], dst.at[it, part], what, slot_of(what, it, phase),
            lax.rem(mine + 1, n),
        )

    started = []

    def start(what, it, phase, src, dst):
        send_all(what, it, phase, src, dst)
        started.append((what, it, phase, src, dst))

    for i, ref in enumerate((c_in, mc_in, vc_in)):
        for d in range(n_all):
            g, h = d // groups, d % groups
            split[i, d] = ref[g * chunk : (g + 1) * chunk, h * LANES : (h + 1) * LANES]

    a = a_in[...]
    b = b_in[...]
    st_a[0], st_a[1], st_a[2] = a, ma_in[...], va_in[...]
    st_b[0], st_b[1], st_b[2] = b, mb_in[...], vb_in[...]
    st_c[0], st_c[1], st_c[2] = split[0, me], split[1, me], split[2, me]
    ag_a[0, col] = a.astype(BF16)
    ag_b[0, row] = b.astype(BF16)
    c_f[...] = c_in[...].astype(BF16).astype(F32)

    pl.semaphore_wait(barrier, n_all - 1)
    start("b", 0, 0, ag_b, ag_b)
    start("a", 0, 0, ag_a, ag_a)
    load_x.wait()
    load_k.wait()

    spread = learn_rate * ITERS
    for it in range(ITERS):
        whole("a", it, 0, ag_a, ag_a).wait_recv()
        whole("b", it, 0, ag_b, ag_b).wait_recv()
        if it > 0:
            whole("c", it, 0, ag_c, ag_c).wait_recv()
            for d in range(n_all):
                g, h = d // groups, d % groups
                c_f[g * chunk : (g + 1) * chunk, h * LANES : (h + 1) * LANES] = (
                    ag_c[it, d].astype(BF16).astype(F32)
                )
        a_f[...] = ag_a[it].reshape(tile_rows, rank).astype(F32)
        bt[...] = ag_b[it].reshape(tile_cols, rank).T
        gb[...] = jnp.zeros_like(gb)
        gc[...] = jnp.zeros_like(gc)

        def block(s, carry):
            at = pl.ds(pl.multiple_of(s * BLOCK, BLOCK), BLOCK)
            a8 = a_f[at, :]
            c3 = c_f[...]
            p = (a8[:, None, :] * c3[None]).astype(BF16).reshape(BLOCK * depth, rank)
            m = jnp.dot(p, bt[...], preferred_element_type=F32)
            x = x_s[at].reshape(BLOCK * depth, tile_cols).astype(F32)
            huber = jnp.clip(m - x, -1.0, 1.0)
            logit = 0.5 * jnp.tanh(0.5 * m) + jnp.where(x > 0, -0.5, 0.5)
            is_logit = jnp.broadcast_to(kind_s[0:1, :], m.shape) == 1
            y = jnp.where(is_logit, logit, huber).astype(BF16)
            z = jnp.dot(
                y, ag_b[it].reshape(tile_cols, rank), preferred_element_type=F32
            ).reshape(BLOCK, depth, rank)
            ga[at, :] = jnp.sum(z * c3[None], axis=1) * scales[0]
            gc[...] += jnp.sum(z * a8[:, None, :], axis=0)
            gb[...] += lax.dot_general(
                y, p, (((0,), (0,)), ((), ())), preferred_element_type=F32
            )
            return carry

        lax.fori_loop(0, tile_rows // BLOCK, block, 0)

        gb[...] = gb[...] * scales[1]
        gs_b[it] = gb[...].astype(BF16).reshape(n_row, own_b, rank)
        start("b", it, 1, gs_b, rs_b)
        for d in range(n_all):
            g, h = d // groups, d % groups
            gs_c[it, d] = (
                gc[g * chunk : (g + 1) * chunk, h * LANES : (h + 1) * LANES] * scales[2]
            )
        start("c", it, 1, gs_c, rs_c)
        gs_a[it] = ga[...].astype(BF16).reshape(n_col, own_a, rank)
        start("a", it, 1, gs_a, rs_a)
        rs_c[it, me] = gs_c[it, me]

        counter = STEP + it + 1
        last = it == ITERS - 1

        def apply(state, grad):
            f, m, v = adam_step(state[0], state[1], state[2], grad, counter)
            state[0], state[1], state[2] = f, m, v
            return f

        whole("c", it, 1, gs_c, rs_c).wait_recv()
        c = apply(st_c, jnp.sum(rs_c[it], axis=0))
        ag_c[it + 1, me] = (split[0, me] - c) / spread if last else c
        start("c", it + 1, 0, ag_c, ag_c)

        whole("b", it, 1, gs_b, rs_b).wait_recv()
        grad = gb[pl.ds(pl.multiple_of(row * own_b, own_b), own_b), :]
        for k in range(1, n_row):
            grad = grad + rs_b[it, lax.rem(row + k, n_row)].astype(F32)
        b = apply(st_b, grad)
        if last:
            ob[...] = (b_in[...] - b) / spread
        else:
            ag_b[it + 1, row] = b.astype(BF16)
            start("b", it + 1, 0, ag_b, ag_b)

        whole("a", it, 1, gs_a, rs_a).wait_recv()
        grad = ga[pl.ds(pl.multiple_of(col * own_a, own_a), own_a), :]
        for k in range(1, n_col):
            grad = grad + rs_a[it, lax.rem(col + k, n_col)].astype(F32)
        a = apply(st_a, grad)
        if last:
            oa[...] = (a_in[...] - a) / spread
        else:
            ag_a[it + 1, col] = a.astype(BF16)
            start("a", it + 1, 0, ag_a, ag_a)

    whole("c", ITERS, 0, ag_c, ag_c).wait_recv()
    for d in range(n_all):
        g, h = d // groups, d % groups
        oc[g * chunk : (g + 1) * chunk, h * LANES : (h + 1) * LANES] = ag_c[ITERS, d]
    for args in started:
        whole(*args).wait_send()


def shards(tensor, loss_kind, a, b, c, ma, va, mb, vb, mc, vc):
    tile_rows, depth, tile_cols = tensor.shape
    rank = a.shape[1]
    n_row = lax.axis_size("row")
    n_col = lax.axis_size("col")
    n_all = n_row * n_col
    full_rows = tile_rows * n_row
    full_cols = tile_cols * n_col
    scales = (
        1.0 / math.sqrt(full_cols * depth),
        1.0 / math.sqrt(full_rows * depth),
        1.0 / math.sqrt(full_rows * full_cols),
    )
    chunk = depth * rank // (n_all * LANES)
    own_a, own_b = a.shape[0], b.shape[0]
    vmem = pl.BlockSpec(memory_space=pltpu.VMEM)
    hbm = pl.BlockSpec(memory_space=pl.ANY)
    slots = 6 * (ITERS + 1)
    return pl.pallas_call(
        functools.partial(kernel, n_row, n_col, scales),
        out_shape=tuple(jax.ShapeDtypeStruct(f.shape, F32) for f in (a, b, c)),
        in_specs=[hbm] * 2 + [vmem] * 9,
        out_specs=[vmem] * 3,
        scratch_shapes=[
            pltpu.VMEM(tensor.shape, tensor.dtype),
            pltpu.VMEM((8, tile_cols), jnp.int32),
            pltpu.VMEM((ITERS, n_col, own_a, rank), BF16),
            pltpu.VMEM((ITERS, n_row, own_b, rank), BF16),
            pltpu.VMEM((ITERS + 1, n_all, chunk, LANES), F32),
            pltpu.VMEM((ITERS, n_col, own_a, rank), BF16),
            pltpu.VMEM((ITERS, n_row, own_b, rank), BF16),
            pltpu.VMEM((ITERS, n_all, chunk, LANES), F32),
            pltpu.VMEM((ITERS, n_col, own_a, rank), BF16),
            pltpu.VMEM((ITERS, n_row, own_b, rank), BF16),
            pltpu.VMEM((ITERS, n_all, chunk, LANES), F32),
            pltpu.VMEM((tile_rows, rank), F32),
            pltpu.VMEM((rank, tile_cols), BF16),
            pltpu.VMEM((depth, rank), F32),
            pltpu.VMEM((tile_rows, rank), F32),
            pltpu.VMEM((tile_cols, rank), F32),
            pltpu.VMEM((depth, rank), F32),
            pltpu.VMEM((3, own_a, rank), F32),
            pltpu.VMEM((3, own_b, rank), F32),
            pltpu.VMEM((3, chunk, LANES), F32),
            pltpu.VMEM((3, n_all, chunk, LANES), F32),
            pltpu.SemaphoreType.DMA((2,)),
            pltpu.SemaphoreType.DMA((slots,)),
            pltpu.SemaphoreType.DMA((slots,)),
        ],
        compiler_params=pltpu.CompilerParams(
            collective_id=0, has_side_effects=True, vmem_limit_bytes=60 * 1024 * 1024
        ),
    )(tensor, loss_kind, a, b, c, ma, va, mb, vb, mc, vc)


def solution(mesh):
    in_specs = (
        P("row", None, "col"),
        P("row", None, "col"),
        P(("row", "col"), None),
        P(("col", "row"), None),
        P(),
        P(("row", "col"), None),
        P(("row", "col"), None),
        P(("col", "row"), None),
        P(("col", "row"), None),
        P(),
        P(),
    )
    out_specs = (P(("row", "col"), None), P(("col", "row"), None), P())
    return jax.shard_map(shards, mesh=mesh, in_specs=in_specs, out_specs=out_specs, check_vma=False)
```

time: 400 us -> 70.6 us (0.18)
  waiting for transfers between devices: 237 us -> 0 us
  blocking collectives: 73.9 us -> 0 us
  Pallas kernels: 0 us -> 65.3 us
  other arithmetic: 39.1 us -> 0 us
  matrix products: 31.8 us -> 0 us
  between operations: 16 us -> 0.64 us
    psum x2 -> x0, waiting for transfers between devices: 236 us -> none  [third_sum(): return lax.psum(grad_three, ('row', 'col'))]
    all_gather x4 -> x0, blocking collectives: 73.9 us -> none  [the longest x2 61.8 us: shards(): lax.all_gather(factor_two.astype(jnp.bfloat16), 'row', axis=0, tiled=True)]
    pallas_call x0 -> x1, Pallas kernels: none -> 65.3 us  [shards(): pl.pallas_call(functools.partial(kernel, n_row, n_col, scales), out_shape...]
    dot_general x6 -> x0, matrix products: 31.8 us -> none  [the longest x2 16.2 us: tile_grads(): jnp.dot(deriv_bf, half_two, preferred_element_type=jnp.float32)]
    reduce_sum x2 -> x0, other arithmetic: 16.8 us -> none  [tile_grads(): grad_three = jnp.sum(projected * one_f[:, None, :], axis=0) * scales[2]]
    convert_element_type x10 -> x0, other arithmetic: 11.9 us -> none  [the longest x2 6.65 us: tile_grads(): scaled_rows = (one_f[:, None, :] * three_f[None, :, :]).astype(jnp.bfloat...]
    div x3 -> x0, other arithmetic: 4.75 us -> none  [the longest x1 1.75 us: shards(): (start_three - factor_three) / spread]
  transfers between devices with their start and end apart: 6 -> 0, of which waited for: 2 -> 0; matrix products, arithmetic and copies ran while one was open for 4% -> 0% of each run, Pallas kernels for 0% -> 0%
where the time goes in v1:
time: 70.6 us; the launch traced here: 70.3 us
  Pallas kernels  65.3 us (92%)
  local copies, waits for them, and re-layouts  4.41 us (6%)
    pallas_call x1, Pallas kernels, shards(): pl.pallas_call(functools.partial(kernel, n_row, n_col, scales), out_shape...  65.3 us
    unnamed x3, local copies, waits for them, and re-layouts  4.41 us

profile of v1, /device:TPU:0, one launch (start us, length us, event | category | flops | bytes accessed | tf_op | source)
XLA Modules:
  0.0 70.3 jit_solution(378408383627149081)
XLA Ops:
  0.6 65.3 %shard_map.130 = (f32[32,512]{1,0:T(8,128)}, f32[16,512]{1,0:T(8,128)}, f32[64,512]{1,0:T(8,128)}) custom-call(bf16[128,64,128]{2,1,0:T(8,128)(2,1)} %tensor.1, s32[128,64,128]{2,1,0:T(8,128)} %kind.1, f32[32,512]{1,0:T(8,128)} %a_in.1, f32[16,512]{1,0:T(8,128)} %b_in.1, f32[64,512]{1,0:T(8,128)} %c_in.1, f32[32,512]{1,0:T(8,128)} %ma_in.1, ...), custom_call_target="tpu_custom_call" | custom-call | tf_op jit(solution)/shard_map/pallas_call | solution.py:245
  65.9 1.5 %copy.17 = f32[32,512]{1,0:T(8,128)} copy(f32[32,512]{1,0:T(8,128)} %get-tuple-element.6) | data formatting | bytes 131072
  67.4 1.4 %copy.18 = f32[16,512]{1,0:T(8,128)} copy(f32[16,512]{1,0:T(8,128)} %get-tuple-element.7) | data formatting | bytes 65536
  68.8 1.6 %copy.19 = f32[64,512]{1,0:T(8,128)} copy(f32[64,512]{1,0:T(8,128)} %get-tuple-element.8) | data formatting | bytes 262144

commit v2 on v1

--- a/solution.py
+++ b/solution.py
@@ -10,7 +10,7 @@
 
 ITERS = 2
 STEP = 10
-BLOCK = 8
+BLOCK = 32
 LANES = 128
 
 learn_rate = 0.05
@@ -47,6 +47,7 @@
     rank = a_f.shape[1]
     own_a = a_in.shape[0]
     own_b = b_in.shape[0]
+    step_rows = min(BLOCK, own_a)
     chunk = st_c.shape[1]
     groups = rank // LANES
 
@@ -145,28 +146,42 @@
         gb[...] = jnp.zeros_like(gb)
         gc[...] = jnp.zeros_like(gc)
 
-        def block(s, carry):
-            at = pl.ds(pl.multiple_of(s * BLOCK, BLOCK), BLOCK)
-            a8 = a_f[at, :]
-            c3 = c_f[...]
-            p = (a8[:, None, :] * c3[None]).astype(BF16).reshape(BLOCK * depth, rank)
-            m = jnp.dot(p, bt[...], preferred_element_type=F32)
-            x = x_s[at].reshape(BLOCK * depth, tile_cols).astype(F32)
-            huber = jnp.clip(m - x, -1.0, 1.0)
-            logit = 0.5 * jnp.tanh(0.5 * m) + jnp.where(x > 0, -0.5, 0.5)
-            is_logit = jnp.broadcast_to(kind_s[0:1, :], m.shape) == 1
-            y = jnp.where(is_logit, logit, huber).astype(BF16)
-            z = jnp.dot(
-                y, ag_b[it].reshape(tile_cols, rank), preferred_element_type=F32
-            ).reshape(BLOCK, depth, rank)
-            ga[at, :] = jnp.sum(z * c3[None], axis=1) * scales[0]
-            gc[...] += jnp.sum(z * a8[:, None, :], axis=0)
-            gb[...] += lax.dot_general(
-                y, p, (((0,), (0,)), ((), ())), preferred_element_type=F32
-            )
+        def owner(t, carry):
+            q = lax.rem(col + 1 + t, n_col)
+            base = pl.multiple_of(q * own_a, own_a)
+
+            def block(s, carry):
+                at = pl.ds(pl.multiple_of(base + s * step_rows, step_rows), step_rows)
+                a8 = a_f[at, :]
+                c3 = c_f[...]
+                p = (a8[:, None, :] * c3[None]).astype(BF16).reshape(step_rows * depth, rank)
+                m = jnp.dot(p, bt[...], preferred_element_type=F32)
+                x = x_s[at].reshape(step_rows * depth, tile_cols).astype(F32)
+                huber = jnp.clip(m - x, -1.0, 1.0)
+                logit = 0.5 * jnp.tanh(0.5 * m) + jnp.where(x > 0, -0.5, 0.5)
+                is_logit = jnp.broadcast_to(kind_s[0:1, :], m.shape) == 1
+                y = jnp.where(is_logit, logit, huber).astype(BF16)
+                z = jnp.dot(
+                    y, ag_b[it].reshape(tile_cols, rank), preferred_element_type=F32
+                ).reshape(step_rows, depth, rank)
+                ga[at, :] = jnp.sum(z * c3[None], axis=1) * scales[0]
+                gc[...] += jnp.sum(z * a8[:, None, :], axis=0)
+                gb[...] += lax.dot_general(
+                    y, p, (((0,), (0,)), ((), ())), preferred_element_type=F32
+                )
+                return carry
+
+            lax.fori_loop(0, own_a // step_rows, block, 0)
+            gs_a[it, q] = ga[pl.ds(base, own_a), :].astype(BF16)
+
+            @pl.when(t < n_col - 1)
+            def _():
+                copy(gs_a.at[it, q], rs_a.at[it, col], "a", slot_of("a", it, 1), q).start()
+
             return carry
 
-        lax.fori_loop(0, tile_rows // BLOCK, block, 0)
+        lax.fori_loop(0, n_col, owner, 0)
+        started.append(("a", it, 1, gs_a, rs_a))
 
         gb[...] = gb[...] * scales[1]
         gs_b[it] = gb[...].astype(BF16).reshape(n_row, own_b, rank)
@@ -175,10 +190,8 @@
             g, h = d // groups, d % groups
             gs_c[it, d] = (
                 gc[g * chunk : (g + 1) * chunk, h * LANES : (h + 1) * LANES] * scales[2]
-            )
+            ).astype(BF16)
         start("c", it, 1, gs_c, rs_c)
-        gs_a[it] = ga[...].astype(BF16).reshape(n_col, own_a, rank)
-        start("a", it, 1, gs_a, rs_a)
         rs_c[it, me] = gs_c[it, me]
 
         counter = STEP + it + 1
@@ -189,8 +202,19 @@
             state[0], state[1], state[2] = f, m, v
             return f
 
+        whole("a", it, 1, gs_a, rs_a).wait_recv()
+        grad = ga[pl.ds(pl.multiple_of(col * own_a, own_a), own_a), :]
+        for k in range(1, n_col):
+            grad = grad + rs_a[it, lax.rem(col + k, n_col)].astype(F32)
+        a = apply(st_a, grad)
+        if last:
+            oa[...] = (a_in[...] - a) / spread
+        else:
+            ag_a[it + 1, col] = a.astype(BF16)
+            start("a", it + 1, 0, ag_a, ag_a)
+
         whole("c", it, 1, gs_c, rs_c).wait_recv()
-        c = apply(st_c, jnp.sum(rs_c[it], axis=0))
+        c = apply(st_c, jnp.sum(rs_c[it].astype(F32), axis=0))
         ag_c[it + 1, me] = (split[0, me] - c) / spread if last else c
         start("c", it + 1, 0, ag_c, ag_c)
 
@@ -205,23 +229,18 @@
             ag_b[it + 1, row] = b.astype(BF16)
             start("b", it + 1, 0, ag_b, ag_b)
 
-        whole("a", it, 1, gs_a, rs_a).wait_recv()
-        grad = ga[pl.ds(pl.multiple_of(col * own_a, own_a), own_a), :]
-        for k in range(1, n_col):
-            grad = grad + rs_a[it, lax.rem(col + k, n_col)].astype(F32)
-        a = apply(st_a, grad)
-        if last:
-            oa[...] = (a_in[...] - a) / spread
-        else:
-            ag_a[it + 1, col] = a.astype(BF16)
-            start("a", it + 1, 0, ag_a, ag_a)
-
     whole("c", ITERS, 0, ag_c, ag_c).wait_recv()
     for d in range(n_all):
         g, h = d // groups, d % groups
         oc[g * chunk : (g + 1) * chunk, h * LANES : (h + 1) * LANES] = ag_c[ITERS, d]
     for args in started:
         whole(*args).wait_send()
+
+
+def hand_on(a, b, c, oa, ob, oc):
+    oa[...] = a[...]
+    ob[...] = b[...]
+    oc[...] = c[...]
 
 
 def shards(tensor, loss_kind, a, b, c, ma, va, mb, vb, mc, vc):
@@ -242,7 +261,7 @@
     vmem = pl.BlockSpec(memory_space=pltpu.VMEM)
     hbm = pl.BlockSpec(memory_space=pl.ANY)
     slots = 6 * (ITERS + 1)
-    return pl.pallas_call(
+    outs = pl.pallas_call(
         functools.partial(kernel, n_row, n_col, scales),
         out_shape=tuple(jax.ShapeDtypeStruct(f.shape, F32) for f in (a, b, c)),
         in_specs=[hbm] * 2 + [vmem] * 9,
@@ -255,10 +274,10 @@
             pltpu.VMEM((ITERS + 1, n_all, chunk, LANES), F32),
             pltpu.VMEM((ITERS, n_col, own_a, rank), BF16),
             pltpu.VMEM((ITERS, n_row, own_b, rank), BF16),
-            pltpu.VMEM((ITERS, n_all, chunk, LANES), F32),
+            pltpu.VMEM((ITERS, n_all, chunk, LANES), BF16),
             pltpu.VMEM((ITERS, n_col, own_a, rank), BF16),
             pltpu.VMEM((ITERS, n_row, own_b, rank), BF16),
-            pltpu.VMEM((ITERS, n_all, chunk, LANES), F32),
+            pltpu.VMEM((ITERS, n_all, chunk, LANES), BF16),
             pltpu.VMEM((tile_rows, rank), F32),
             pltpu.VMEM((rank, tile_cols), BF16),
             pltpu.VMEM((depth, rank), F32),
@@ -277,6 +296,12 @@
             collective_id=0, has_side_effects=True, vmem_limit_bytes=60 * 1024 * 1024
         ),
     )(tensor, loss_kind, a, b, c, ma, va, mb, vb, mc, vc)
+    return pl.pallas_call(
+        hand_on,
+        out_shape=tuple(jax.ShapeDtypeStruct(f.shape, F32) for f in (a, b, c)),
+        in_specs=[vmem] * 3,
+        out_specs=[vmem] * 3,
+    )(*outs)
 
 
 def solution(mesh):

time: 70.6 us -> 60 us (0.85)
  Pallas kernels: 65.3 us -> 59.2 us
  local copies, waits for them, and re-layouts: 4.41 us -> 0 us
    pallas_call x1, Pallas kernels: 65.3 us -> 57.6 us  [shards(): pl.pallas_call(functools.partial(kernel, n_row, n_col, scales), out_shape...]
    unnamed x3 -> x0, local copies, waits for them, and re-layouts: 4.41 us -> none
    pallas_call x0 -> x1, Pallas kernels: none -> 1.65 us  [shards(): pl.pallas_call(hand_on, out_shape=tuple((jax.ShapeDtypeStruct(f.shape, F3...]
where the time goes in v2:
time: 60 us; the launch traced here: 59.8 us
  Pallas kernels  59.2 us (99%)
  between operations  0.64 us (1%)
    pallas_call x1, Pallas kernels, shards(): pl.pallas_call(functools.partial(kernel, n_row, n_col, scales), out_shape...  57.6 us
    pallas_call x1, Pallas kernels, shards(): pl.pallas_call(hand_on, out_shape=tuple((jax.ShapeDtypeStruct(f.shape, F3...  1.65 us

profile of v2, /device:TPU:0, one launch (start us, length us, event | category | flops | bytes accessed | tf_op | source)
XLA Modules:
  0.0 59.8 jit_solution(5096758679201056887)
XLA Ops:
  0.6 57.6 %shard_map.130 = (f32[32,512]{1,0:T(8,128)}, f32[16,512]{1,0:T(8,128)}, f32[64,512]{1,0:T(8,128)}) custom-call(bf16[128,64,128]{2,1,0:T(8,128)(2,1)} %tensor.1, s32[128,64,128]{2,1,0:T(8,128)} %kind.1, f32[32,512]{1,0:T(8,128)} %a_in.1, f32[16,512]{1,0:T(8,128)} %b_in.1, f32[64,512]{1,0:T(8,128)} %c_in.1, f32[32,512]{1,0:T(8,128)} %ma_in.1, ...), custom_call_target="tpu_custom_call" | custom-call | tf_op jit(solution)/shard_map/pallas_call | solution.py:264
  58.2 1.7 %shard_map.131 = (f32[32,512]{1,0:T(8,128)}, f32[16,512]{1,0:T(8,128)}, f32[64,512]{1,0:T(8,128)}) custom-call(f32[32,512]{1,0:T(8,128)} %get-tuple-element.6.a, f32[16,512]{1,0:T(8,128)} %get-tuple-element.7.b, f32[64,512]{1,0:T(8,128)} %get-tuple-element.8.c), custom_call_target="tpu_custom_call" | custom-call | tf_op jit(solution)/shard_map/pallas_call | solution.py:299

commit v3 on v2

--- a/solution.py
+++ b/solution.py
@@ -33,10 +33,11 @@
 
 def kernel(
     n_row, n_col, scales,
-    tensor, kind, a_in, b_in, c_in, ma_in, va_in, mb_in, vb_in, mc_in, vc_in,
+    tensor, kind, a_hbm, b_hbm, c_hbm, ma_hbm, va_hbm, mb_hbm, vb_hbm, mc_hbm, vc_hbm,
     oa, ob, oc,
     x_s, kind_s, ag_a, ag_b, ag_c, gs_a, gs_b, gs_c, rs_a, rs_b, rs_c,
-    a_f, bt, c_f, ga, gb, gc, st_a, st_b, st_c, split,
+    a_f, bt, c_f, ga, gb, gc, st_a, st_b, st_c, split, p_s, y_s,
+    a_in, b_in, c_in, ma_in, va_in, mb_in, vb_in, mc_in, vc_in,
     load_sem, sends, recvs,
 ):
     row = lax.axis_index("row")
@@ -48,13 +49,24 @@
     own_a = a_in.shape[0]
     own_b = b_in.shape[0]
     step_rows = min(BLOCK, own_a)
+    second_rows = BLOCK * depth
     chunk = st_c.shape[1]
     groups = rank // LANES
 
     load_x = pltpu.make_async_copy(tensor, x_s, load_sem.at[0])
+    load_k = pltpu.make_async_copy(kind.at[0, pl.ds(0, 8)], kind_s, load_sem.at[1])
+
+    pairs = (
+        (a_hbm, a_in), (b_hbm, b_in), (c_hbm, c_in), (ma_hbm, ma_in), (va_hbm, va_in),
+        (mb_hbm, mb_in), (vb_hbm, vb_in), (mc_hbm, mc_in), (vc_hbm, vc_in),
+    )
+    loads = [
+        pltpu.make_async_copy(src, dst, load_sem.at[2 + i]) for i, (src, dst) in enumerate(pairs)
+    ]
+    for load in loads:
+        load.start()
+    load_k.start()
     load_x.start()
-    load_k = pltpu.make_async_copy(kind.at[0, pl.ds(0, 8)], kind_s, load_sem.at[1])
-    load_k.start()
 
     barrier = pltpu.get_barrier_semaphore()
 
@@ -110,6 +122,8 @@
         send_all(what, it, phase, src, dst)
         started.append((what, it, phase, src, dst))
 
+    for load in loads:
+        load.wait()
     for i, ref in enumerate((c_in, mc_in, vc_in)):
         for d in range(n_all):
             g, h = d // groups, d % groups
@@ -155,6 +169,10 @@
                 a8 = a_f[at, :]
                 c3 = c_f[...]
                 p = (a8[:, None, :] * c3[None]).astype(BF16).reshape(step_rows * depth, rank)
+                span = pl.ds(
+                    pl.multiple_of((base + s * step_rows) * depth, step_rows * depth), step_rows * depth
+                )
+                p_s[span, :] = p
                 m = jnp.dot(p, bt[...], preferred_element_type=F32)
                 x = x_s[at].reshape(step_rows * depth, tile_cols).astype(F32)
                 huber = jnp.clip(m - x, -1.0, 1.0)
@@ -166,9 +184,7 @@
                 ).reshape(step_rows, depth, rank)
                 ga[at, :] = jnp.sum(z * c3[None], axis=1) * scales[0]
                 gc[...] += jnp.sum(z * a8[:, None, :], axis=0)
-                gb[...] += lax.dot_general(
-                    y, p, (((0,), (0,)), ((), ())), preferred_element_type=F32
-                )
+                y_s[span, :] = y
                 return carry
 
             lax.fori_loop(0, own_a // step_rows, block, 0)
@@ -183,9 +199,6 @@
         lax.fori_loop(0, n_col, owner, 0)
         started.append(("a", it, 1, gs_a, rs_a))
 
-        gb[...] = gb[...] * scales[1]
-        gs_b[it] = gb[...].astype(BF16).reshape(n_row, own_b, rank)
-        start("b", it, 1, gs_b, rs_b)
         for d in range(n_all):
             g, h = d // groups, d % groups
             gs_c[it, d] = (
@@ -193,6 +206,18 @@
             ).astype(BF16)
         start("c", it, 1, gs_c, rs_c)
         rs_c[it, me] = gs_c[it, me]
+
+        def second(s, carry):
+            span = pl.ds(pl.multiple_of(s * second_rows, second_rows), second_rows)
+            gb[...] += lax.dot_general(
+                y_s[span, :], p_s[span, :], (((0,), (0,)), ((), ())), preferred_element_type=F32
+            )
+            return carry
+
+        lax.fori_loop(0, tile_rows * depth // second_rows, second, 0)
+        gb[...] = gb[...] * scales[1]
+        gs_b[it] = gb[...].astype(BF16).reshape(n_row, own_b, rank)
+        start("b", it, 1, gs_b, rs_b)
 
         counter = STEP + it + 1
         last = it == ITERS - 1
@@ -264,7 +289,7 @@
     outs = pl.pallas_call(
         functools.partial(kernel, n_row, n_col, scales),
         out_shape=tuple(jax.ShapeDtypeStruct(f.shape, F32) for f in (a, b, c)),
-        in_specs=[hbm] * 2 + [vmem] * 9,
+        in_specs=[hbm] * 11,
         out_specs=[vmem] * 3,
         scratch_shapes=[
             pltpu.VMEM(tensor.shape, tensor.dtype),
@@ -288,7 +313,10 @@
             pltpu.VMEM((3, own_b, rank), F32),
             pltpu.VMEM((3, chunk, LANES), F32),
             pltpu.VMEM((3, n_all, chunk, LANES), F32),
-            pltpu.SemaphoreType.DMA((2,)),
+            pltpu.VMEM((tile_rows * depth, rank), BF16),
+            pltpu.VMEM((tile_rows * depth, tile_cols), BF16),
+            *[pltpu.VMEM(f.shape, F32) for f in (a, b, c, ma, va, mb, vb, mc, vc)],
+            pltpu.SemaphoreType.DMA((11,)),
             pltpu.SemaphoreType.DMA((slots,)),
             pltpu.SemaphoreType.DMA((slots,)),
         ],

time: 60 us -> 54.4 us (0.907)
  Pallas kernels: 59.2 us -> 53.6 us
    pallas_call x1, Pallas kernels: 57.6 us -> 51.9 us  [shards(): pl.pallas_call(functools.partial(kernel, n_row, n_col, scales), out_shape...]
where the time goes in v3:
time: 54.4 us; the launch traced here: 54.2 us
  Pallas kernels  53.6 us (99%)
  between operations  0.64 us (1%)
    pallas_call x1, Pallas kernels, shards(): pl.pallas_call(functools.partial(kernel, n_row, n_col, scales), out_shape...  51.9 us
    pallas_call x1, Pallas kernels, shards(): pl.pallas_call(hand_on, out_shape=tuple((jax.ShapeDtypeStruct(f.shape, F3...  1.65 us

profile of v3, /device:TPU:0, one launch (start us, length us, event | category | flops | bytes accessed | tf_op | source)
XLA Modules:
  0.0 54.2 jit_solution(3492931410007918595)
XLA Ops:
  0.6 51.9 %shard_map.130 = (f32[32,512]{1,0:T(8,128)}, f32[16,512]{1,0:T(8,128)}, f32[64,512]{1,0:T(8,128)}) custom-call(bf16[128,64,128]{2,1,0:T(8,128)(2,1)} %tensor.1, s32[128,64,128]{2,1,0:T(8,128)} %kind.1, f32[32,512]{1,0:T(8,128)} %a_hbm.1, f32[16,512]{1,0:T(8,128)} %b_hbm.1, f32[64,512]{1,0:T(8,128)} %c_hbm.1, f32[32,512]{1,0:T(8,128)} %ma_hbm.1, ...), custom_call_target="tpu_custom_call" | custom-call | tf_op jit(solution)/shard_map/pallas_call | solution.py:289
  52.6 1.7 %shard_map.131 = (f32[32,512]{1,0:T(8,128)}, f32[16,512]{1,0:T(8,128)}, f32[64,512]{1,0:T(8,128)}) custom-call(f32[32,512]{1,0:T(8,128)} %get-tuple-element.6.a, f32[16,512]{1,0:T(8,128)} %get-tuple-element.7.b, f32[64,512]{1,0:T(8,128)} %get-tuple-element.8.c), custom_call_target="tpu_custom_call" | custom-call | tf_op jit(solution)/shard_map/pallas_call | solution.py:327
